TPU v7x, 256 devices: a whole 4x4x8 slice. The times are simulated.
256 devices in a mesh: ctx: 8 (over z), head: 32 (over y, x, core).
Axes of the slice: x: 4, y: 4, z: 8, core: 2. Of those that a mesh axis runs over, the one named last changes fastest.
Arguments:
- hidden: float32 [2048, 2304], P(('ctx', 'head')), may hold values from -40 to 40
- w_query: float32 [2304, 6144], P(None, 'head'), may hold values from -0.125 to 0.125
- w_down: float32 [2304, 576], replicated, may hold values from -0.125 to 0.125
- latent_gain: float32 [512], replicated, may hold values from 0.25 to 1.75
- w_key_up: float32 [512, 4096], P(None, 'head'), may hold values from -0.25 to 0.25
- w_value_up: float32 [512, 4096], P(None, 'head'), may hold values from -0.25 to 0.25
- w_out: float32 [4096, 2304], P('head'), may hold values from -0.09375 to 0.09375
Outputs:
- output: float32 [2048, 2304], P(('ctx', 'head'))
All inputs are finite; a program needn't handle non-finite values.
Results may differ from a plain program's by a relative error of at most 0.0003.
Values sent between devices are 32-bit elements; how exact they have to be, the bound alone decides.
No kernel may reach another device: no remote copies, remote signals or barrier semaphores. Data moves between devices by JAX's collectives and lax.ppermute only.
A program may use at most 64 MiB of HBM per device.

v0:
```python
import jax
import jax.numpy as jnp
from jax import lax
from jax.sharding import PartitionSpec as P

EXACT = lax.Precision.HIGHEST
EPSILON = 1e-06
FLOOR = -1e30


def in_order(pieces, dim):
    pieces = jnp.moveaxis(pieces, 0, dim)
    shape = pieces.shape
    return pieces.reshape(*shape[:dim], shape[dim] * shape[dim + 1], *shape[dim + 2 :])


def copy_for_each(array, axis):
    copies = jnp.broadcast_to(array, (lax.axis_size(axis), *array.shape))
    return lax.all_to_all(copies, axis, split_axis=0, concat_axis=0, tiled=True)


def gather_directly(array, axis, dim):
    return in_order(copy_for_each(array, axis), dim)


def in_blocks(array, dim, size):
    shape = array.shape
    pieces = array.reshape(*shape[:dim], size, shape[dim] // size, *shape[dim + 1 :])
    return jnp.moveaxis(pieces, dim, 0)


def summed_on_arrival(array, axis, dim):
    pieces = in_blocks(array, dim, lax.axis_size(axis))
    arrived = lax.all_to_all(pieces, axis, split_axis=0, concat_axis=0, tiled=True)
    return arrived.sum(axis=0)


def matmul(left, right):
    return jnp.dot(left, right, precision=EXACT, preferred_element_type=jnp.float32)


def on_device(hidden, w_query, w_down, latent_gain, w_key_up, w_value_up, w_out):
    rank = w_key_up.shape[0]
    nope = w_key_up.shape[1]
    down_part = matmul(hidden, w_down)
    raw_latent = down_part[:, :rank]
    meansq = jnp.mean(raw_latent * raw_latent, axis=-1, keepdims=True)
    own_latent = jnp.concatenate(
        [raw_latent * lax.rsqrt(meansq + EPSILON) * latent_gain, down_part[:, rank:]], axis=1
    )
    latent_block = gather_directly(own_latent, "head", 0)
    queries = matmul(lax.all_gather(hidden, "head", axis=0, tiled=True), w_query)
    row_count = queries.shape[0]
    score_scale = queries.shape[1] ** (-0.5)
    query_pos = lax.axis_index("ctx") * row_count + jnp.arange(row_count, dtype=jnp.int32)
    latent_part = latent_block[:, :rank]
    projected = jnp.concatenate(
        [matmul(latent_part, w_key_up), latent_block[:, rank:], matmul(latent_part, w_value_up)],
        axis=1,
    )
    shared_end = nope + latent_block.shape[1] - rank
    portion = lax.all_gather(projected, "ctx", axis=0, tiled=True)
    key_own = portion[:, :nope]
    maxima = jnp.full((row_count,), FLOOR, jnp.float32)
    scores = (
        matmul(queries[:, :nope], key_own.T)
        + matmul(queries[:, nope:], portion[:, nope:shared_end].T)
    ) * score_scale
    key_pos = jnp.arange(key_own.shape[0], dtype=jnp.int32)
    causal = query_pos[:, None] >= key_pos[None, :]
    scores = jnp.where(causal, scores, FLOOR)
    new_max = jnp.maximum(maxima, jnp.max(scores, axis=1))
    weights = jnp.where(causal, jnp.exp(scores - new_max[:, None]), 0.0)
    attended = matmul(weights, portion[:, shared_end:]) / jnp.sum(weights, axis=1)[:, None]
    return summed_on_arrival(matmul(attended, w_out), "head", 0)


def solution(mesh):
    placed = (
        P(("ctx", "head"), None),
        P(None, "head"),
        P(),
        P(),
        P(None, "head"),
        P(None, "head"),
        P("head", None),
    )
    return jax.shard_map(
        on_device, mesh=mesh, in_specs=placed, out_specs=P(("ctx", "head"), None), check_vma=False
    )
```

profile of v0, /device:TPU:1, one launch (start us, length us, event | category | flops | bytes accessed | tf_op | source)
XLA Modules:
  0.0 167.0 jit_solution(1022464244086564012)
XLA Ops:
  6.5 0.0 copy-start
  6.5 0.0 all-gather.3.cloned.1.call-start
  6.5 0.7 all-gather.3.cloned.1.call-update
  7.3 0.0 copy-start.5
  7.3 0.0 all-gather.5.cloned.1.call-start
  7.3 6.9 %fusion.21 = f32[8,576]{1,0:T(8,128)S(1)} fusion(f32[8,2304]{1,0:T(8,128)} %param.7, f32[2304,576]{0,1:T(8,128)} %param.9), kind=kOutput, calls=%fused_computation.32 | convolution fusion | flops 127401984 | bytes 5400576 | tf_op jit(solution)/shard_map/dot_general | solution.py:39
  14.2 0.0 copy-start.3
  14.2 0.0 copy-start.4
  14.2 0.1 multiply_reduce_fusion
  14.3 0.0 copy-done.5
  14.4 0.1 multiply_multiply_fusion
  14.5 22.0 %all_to_all.10 = f32[32,8,576]{2,1,0:T(8,128)S(1)} all-to-all(f32[32,8,576]{2,1,0:T(8,128)S(1)} %broadcast_in_dim.19), channel_id=1, replica_groups=mesh['ctx'=8,'head'=32] {'head'}, dimensions={0} | all-to-all | bytes 1179648 | tf_op jit(solution)/shard_map/all_to_all | solution.py:19
  36.5 0.1 copy.10
  36.6 0.0 copy-done.3
  36.6 0.6 fusion.12
  37.2 0.0 copy-done.4
  37.2 0.6 fusion.14
  37.8 0.8 pad_maximum_fusion
  38.6 0.0 all-gather.5.cloned.1.call-update
  38.6 26.6 %all-gather.3.cloned.1.call-done = f32[256,2304]{1,0:T(8,128)} async-done(((f32[8,2304]{1,0:T(8,128)}), f32[256,2304]{1,0:T(8,128)}) %all-gather.3.cloned.1.call-update) | async-done | bytes 2359312 | tf_op jit(solution)/shard_map/all_gather | solution.py:52
  65.3 0.0 copy-done
  65.3 4.1 %fusion.20 = f32[256,192]{0,1:T(8,128)S(1)} fusion(f32[256,2304]{1,0:T(8,128)} %all-gather.3.cloned.1.call-done, f32[2304,192]{0,1:T(8,128)S(1)} %copy-done), kind=kOutput, calls=%fused_computation.31 | convolution fusion | flops 1358954496 | bytes 4325376 | tf_op jit(solution)/shard_map/dot_general | solution.py:39
  69.4 36.0 %all-gather.5.cloned.1.call-done = f32[2048,320]{0,1:T(8,128)} async-done(((f32[256,320]{0,1:T(8,128)}), f32[2048,320]{0,1:T(8,128)}) %all-gather.5.cloned.1.call-update) | async-done | bytes 2621456 | tf_op jit(solution)/shard_map/all_gather | solution.py:62
  105.5 0.0 copy-start.2
  105.5 3.2 %fusion.6 = f32[256,2048]{1,0:T(8,128)S(1)} fusion(f32[2048,320]{0,1:T(8,128)} %all-gather.5.cloned.1.call-done, f32[256,192]{0,1:T(8,128)S(1)} %fusion.20), kind=kOutput, calls=%fused_computation.10 | convolution fusion | flops 805306368 | bytes 3276800 | tf_op jit(solution)/shard_map/dot_general | solution.py:39
  108.7 0.0 copy-done.2
  108.7 2.3 %fusion.19 = (f32[256]{0:T(256)S(1)}, f32[256,2048]{1,0:T(8,128)S(1)}) fusion(f32[256,2048]{1,0:T(8,128)S(1)} %fusion.6, f32[2048,320]{0,1:T(8,128)S(1)} %copy-done.2, f32[256,192]{0,1:T(8,128)S(1)} %fusion.20, s32[256]{0:T(256)S(1)} %iota_add_fusion), kind=kOutput, calls=%fused_computation.30 | convolution fusion | flops 405274368 | bytes 4786176 | tf_op jit(solution)/shard_map/dot_general | solution.py:39
  111.0 0.6 fusion.2
  111.6 0.0 copy-start.1
  111.7 2.2 %fusion.4 = f32[256,128]{1,0:T(8,128)S(1)} fusion(f32[256,2048]{1,0:T(8,128)S(1)} %get-tuple-element.6, f32[2048,320]{0,1:T(8,128)S(1)} %copy-done.2, f32[256]{0:T(256)S(1)} %broadcast_maximum_fusion, s32[256]{0:T(256)S(1)} %iota_add_fusion, f32[256]{0:T(256)S(1)} %fusion.2), kind=kOutput, calls=%fused_computation.8 | convolution fusion | flops 806912000 | bytes 3279872 | tf_op jit(solution)/shard_map/dot_general | solution.py:39
  113.8 0.0 copy-done.1
  113.9 2.0 %convolution_bitcast_fusion = f32[32,8,2304]{2,1,0:T(8,128)S(1)} fusion(f32[256,128]{1,0:T(8,128)S(1)} %fusion.4, f32[128,2304]{1,0:T(8,128)S(1)} %copy-done.1), kind=kOutput, calls=%fused_computation | convolution fusion | flops 905969664 | bytes 3670016 | tf_op jit(solution)/shard_map/dot_general | solution.py:39
  115.9 41.8 %all_to_all.11 = f32[32,8,2304]{2,1,0:T(8,128)} all-to-all(f32[32,8,2304]{2,1,0:T(8,128)S(1)} %convolution_bitcast_fusion), channel_id=1, replica_groups=mesh['ctx'=8,'head'=32] {'head'}, dimensions={0} | all-to-all | bytes 4718592 | tf_op jit(solution)/shard_map/all_to_all | solution.py:34
  157.7 2.4 %reduce_sum.29 = f32[8,2304]{1,0:T(8,128)} reduce(f32[32,8,2304]{2,1,0:T(8,128)} %all_to_all.11, f32[]{:T(128)} %constant.5.clone.1), dimensions={0}, to_apply=%region_3.4 | reduce | flops 571392 | bytes 2433028 | tf_op jit(solution)/shard_map/reduce_sum | solution.py:35
  (7 shorter events, 0.1 us)
Async XLA Ops:
  6.5 58.8 %copy-start = (f32[2304,192]{0,1:T(8,128)S(1)}, f32[2304,192]{0,1:T(8,128)}, u32[]{:S(2)}) copy-start(f32[2304,192]{0,1:T(8,128)} %param.8) | copy-start | bytes 5308420
  6.5 58.8 %all-gather.3.cloned.1.call-start = ((), (), s32[]{:S(2)}) async-start(), calls=%async_computation.2 | async-start | bytes 2433024 | tf_op jit(solution)/shard_map/all_gather | solution.py:52
  7.3 7.1 %copy-start.5 = (f32[512]{0:T(512)S(1)}, f32[512]{0:T(512)}, u32[]{:S(2)}) copy-start(f32[512]{0:T(512)} %param.10) | copy-start | bytes 6148
  7.3 98.2 %all-gather.5.cloned.1.call-start = ((), (), s32[]{:S(2)}) async-start(), calls=%async_computation.3 | async-start | bytes 2949120 | tf_op jit(solution)/shard_map/all_gather | solution.py:62
  14.2 22.4 %copy-start.3 = (f32[512,128]{1,0:T(8,128)S(1)}, f32[512,128]{1,0:T(8,128)}, u32[]{:S(2)}) copy-start(f32[512,128]{1,0:T(8,128)} %param.12) | copy-start | bytes 786436
  14.2 23.1 %copy-start.4 = (f32[512,128]{1,0:T(8,128)S(1)}, f32[512,128]{1,0:T(8,128)}, u32[]{:S(2)}) copy-start(f32[512,128]{1,0:T(8,128)} %param.11) | copy-start | bytes 786436
  105.5 3.2 %copy-start.2 = (f32[2048,320]{0,1:T(8,128)S(1)}, f32[2048,320]{0,1:T(8,128)}, u32[]{:S(2)}) copy-start(f32[2048,320]{0,1:T(8,128)} %all-gather.5.cloned.1.call-done) | copy-start | bytes 7864324
  111.6 2.2 %copy-start.1 = (f32[128,2304]{1,0:T(8,128)S(1)}, f32[128,2304]{1,0:T(8,128)}, u32[]{:S(2)}) copy-start(f32[128,2304]{1,0:T(8,128)} %param.13) | copy-start | bytes 3538948
Sparse Core Ops, SparseCore 0:
  9.9 55.3 all-gather.2
  67.1 38.3 all-gather.4
where the time goes:
time: 167 us
  blocking collectives  63.9 us (38%)
  waiting for transfers between devices  63.4 us (38%)
  matrix products  21.9 us (13%)
  between operations  13.5 us (8%)
  other arithmetic  4.02 us (2%)
    all_to_all x1, blocking collectives, summed_on_arrival(): lax.all_to_all(pieces, axis, split_axis=0, concat_axis=0, tiled=True)  41.8 us
    all_gather x1, waiting for transfers between devices, on_device(): portion = lax.all_gather(projected, 'ctx', axis=0, tiled=True)  36 us
    all_gather x1, waiting for transfers between devices, on_device(): lax.all_gather(hidden, 'head', axis=0, tiled=True)  26.6 us
    all_to_all x1, blocking collectives, copy_for_each(): return lax.all_to_all(copies, axis, split_axis=0, concat_axis=0, tiled=True)  22 us
    dot_general x8, matrix products, matmul(): jnp.dot(left, right, precision=EXACT, preferred_element_type=jnp.float32)  21.9 us
  transfers between devices with their start and end apart: 2, of which 2 were waited for; matrix products, arithmetic and copies ran while one was open for 8% of the time, Pallas kernels for 0%

commit v1 on v0

--- a/solution.py
+++ b/solution.py
@@ -59,7 +59,26 @@
         axis=1,
     )
     shared_end = nope + latent_block.shape[1] - rank
-    portion = lax.all_gather(projected, "ctx", axis=0, tiled=True)
+    peers, index, rows = (lax.axis_size("ctx"), lax.axis_index("ctx"), projected.shape[0])
+    right_2 = [(i, (i + 1) % peers) for i in range(peers)]
+    backward = [(i, (i - 1) % peers) for i in range(peers)]
+    result = jnp.zeros(
+        (*projected.shape[:0], peers * rows, *projected.shape[0 + 1 :]), projected.dtype
+    )
+    result = lax.dynamic_update_slice_in_dim(result, projected, index * rows, axis=0)
+    from_left = from_right = projected
+    middle = peers // 2
+    for lap in range(1, middle + 1):
+        from_left = lax.ppermute(from_left, "ctx", right_2)
+        result = lax.dynamic_update_slice_in_dim(
+            result, from_left, (index - lap) % peers * rows, axis=0
+        )
+        if lap < peers - middle:
+            from_right = lax.ppermute(from_right, "ctx", backward)
+            result = lax.dynamic_update_slice_in_dim(
+                result, from_right, (index + lap) % peers * rows, axis=0
+            )
+    portion = result
     key_own = portion[:, :nope]
     maxima = jnp.full((row_count,), FLOOR, jnp.float32)
     scores = (

time: 167 us -> 149 us (0.89)
  waiting for transfers between devices: 63.4 us -> 36.3 us
  blocking collectives: 63.9 us -> 42.1 us
  starting transfers between devices: 0.04 us -> 19.7 us
  local copies, waits for them, and re-layouts: 0.19 us -> 8.44 us
  matrix products: 21.9 us -> 24.1 us
    all_gather x1 -> x0, waiting for transfers between devices: 36 us -> none  [on_device(): portion = lax.all_gather(projected, 'ctx', axis=0, tiled=True)]
    all_gather x1, waiting for transfers between devices: 26.6 us -> 0.01 us  [on_device(): lax.all_gather(hidden, 'head', axis=0, tiled=True)]
    all_to_all x1 -> x0, blocking collectives: 22 us -> none  [copy_for_each(): return lax.all_to_all(copies, axis, split_axis=0, concat_axis=0, tiled=True)]
    ppermute x0 -> x7, waiting for transfers between devices: none -> 21.9 us  [the longest x4 21.8 us: on_device(): from_left = lax.ppermute(from_left, 'ctx', right_2)]
    all_to_all x0 -> x1, waiting for transfers between devices: none -> 13.7 us  [copy_for_each(): return lax.all_to_all(copies, axis, split_axis=0, concat_axis=0, tiled=True)]
    ppermute x0 -> x7, starting transfers between devices: none -> 11.1 us  [the longest x3 9.51 us: on_device(): from_right = lax.ppermute(from_right, 'ctx', backward)]
    all_to_all x0 -> x1, starting transfers between devices: none -> 8.59 us  [copy_for_each(): return lax.all_to_all(copies, axis, split_axis=0, concat_axis=0, tiled=True)]
    dynamic_update_slice x0 -> x7, local copies, waits for them, and re-layouts: none -> 5.58 us  [the longest x4 3.2 us: on_device(): lax.dynamic_update_slice_in_dim(result, from_left, (index - lap) % peers...]
  transfers between devices with their start and end apart: 2 -> 9, of which waited for: 2 -> 5; matrix products, arithmetic and copies ran while one was open for 8% -> 12% of each run, Pallas kernels for 0% -> 0%
where the time goes in v1:
time: 149 us; the launch traced here: 148 us
  blocking collectives  42.1 us (28%)
  waiting for transfers between devices  36.3 us (24%)
  matrix products  24.1 us (16%)
  starting transfers between devices  19.7 us (13%)
  between operations  13.5 us (9%)
  local copies, waits for them, and re-layouts  8.44 us (6%)
  other arithmetic  4.09 us (3%)
    all_to_all x1, blocking collectives, summed_on_arrival(): lax.all_to_all(pieces, axis, split_axis=0, concat_axis=0, tiled=True)  42.1 us
    dot_general x8, matrix products, matmul(): jnp.dot(left, right, precision=EXACT, preferred_element_type=jnp.float32)  24.1 us
    ppermute x4, waiting for transfers between devices, on_device(): from_left = lax.ppermute(from_left, 'ctx', right_2)  21.8 us
    all_to_all x1, waiting for transfers between devices, copy_for_each(): return lax.all_to_all(copies, axis, split_axis=0, concat_axis=0, tiled=True)  13.7 us
    ppermute x3, starting transfers between devices, on_device(): from_right = lax.ppermute(from_right, 'ctx', backward)  9.51 us
    all_to_all x1, starting transfers between devices, copy_for_each(): return lax.all_to_all(copies, axis, split_axis=0, concat_axis=0, tiled=True)  8.59 us
    dynamic_update_slice x4, local copies, waits for them, and re-layouts, on_device(): lax.dynamic_update_slice_in_dim(result, from_left, (index - lap) % peers...  3.2 us
  transfers between devices with their start and end apart: 9, of which 5 were waited for; matrix products, arithmetic and copies ran while one was open for 12% of the time, Pallas kernels for 0%

profile of v1, /device:TPU:1, one launch (start us, length us, event | category | flops | bytes accessed | tf_op | source)
XLA Modules:
  0.0 148.3 jit_solution(4199987955575818170)
XLA Ops:
  6.5 0.0 copy-start
  6.5 0.0 all-gather.2.cloned.1.call-start
  6.5 0.7 all-gather.2.cloned.1.call-update
  7.3 0.0 copy-start.4
  7.3 6.9 %fusion.21 = f32[8,576]{1,0:T(8,128)S(1)} fusion(f32[8,2304]{1,0:T(8,128)} %param.7, f32[2304,576]{0,1:T(8,128)} %param.9), kind=kOutput, calls=%fused_computation.40 | convolution fusion | flops 127401984 | bytes 5400576 | tf_op jit(solution)/shard_map/dot_general | solution.py:39
  14.2 0.1 multiply_reduce_fusion
  14.3 0.0 copy-done.4
  14.3 0.1 multiply_multiply_fusion
  14.4 0.9 broadcast_in_dim.23
  15.3 8.6 %all-to-all-start = ((f32[32,8,576]{2,1,0:T(8,128)}), f32[32,8,576]{2,1,0:T(8,128)S(1)}, u32[]{:S(2)}, u32[]{:S(2)}) async-start(f32[32,8,576]{2,1,0:T(8,128)} %broadcast_in_dim.23), calls=%async_computation | async-start | bytes 1310720 | tf_op jit(solution)/shard_map/all_to_all | solution.py:19
  23.9 13.7 %all-to-all-done = f32[32,8,576]{2,1,0:T(8,128)S(1)} async-done(((f32[32,8,576]{2,1,0:T(8,128)}), f32[32,8,576]{2,1,0:T(8,128)S(1)}, u32[]{:S(2)}, u32[]{:S(2)}) %all-to-all-start) | async-done | bytes 589856 | tf_op jit(solution)/shard_map/all_to_all | solution.py:19
  37.6 0.1 copy.10
  37.7 0.0 copy-done.2
  37.7 0.6 fusion.12
  38.3 0.0 copy-done.3
  38.3 0.6 fusion.14
  38.9 1.8 %broadcast_in_dim.22 = f32[2048,320]{0,1:T(8,128)} broadcast(f32[]{:T(128)} %constant.61.clone.1), dimensions={} | broadcast | bytes 2621444 | tf_op jit(solution)/shard_map/broadcast_in_dim | solution.py:65
  40.7 0.8 pad_maximum_fusion
  41.6 1.6 %collective-permute-start = (f32[256,320]{0,1:T(8,128)S(1)}, f32[256,320]{0,1:T(8,128)S(1)}, u32[]{:S(2)}, u32[]{:S(2)}) collective-permute-start(f32[256,320]{0,1:T(8,128)S(1)} %get-tuple-element.5), channel_id=1, source_target_pairs={{0,32},{32,64},{64,96},{96,128},{128,160},{160,192},{192,224},{224... | collective-permute-start | bytes 983048 | tf_op jit(solution)/shard_map/ppermute | solution.py:72
  43.2 4.1 %collective-permute-start.1 = (f32[256,320]{0,1:T(8,128)S(1)}, f32[256,320]{0,1:T(8,128)S(1)}, u32[]{:S(2)}, u32[]{:S(2)}) collective-permute-start(f32[256,320]{0,1:T(8,128)S(1)} %get-tuple-element.5), channel_id=1, source_target_pairs={{0,224},{32,0},{64,32},{96,64},{128,96},{160,128},{192,160},{224,1... | collective-permute-start | bytes 983048 | tf_op jit(solution)/shard_map/ppermute | solution.py:77
  47.3 7.4 %collective-permute-done = f32[256,320]{0,1:T(8,128)S(1)} collective-permute-done((f32[256,320]{0,1:T(8,128)S(1)}, f32[256,320]{0,1:T(8,128)S(1)}, u32[]{:S(2)}, u32[]{:S(2)}) %collective-permute-start) | collective-permute-done | bytes 327712 | tf_op jit(solution)/shard_map/ppermute | solution.py:72
  54.7 0.0 collective-permute-start.2
  54.7 0.0 collective-permute-done.1
  54.7 2.7 %collective-permute-start.3 = (f32[256,320]{0,1:T(8,128)S(1)}, f32[256,320]{0,1:T(8,128)S(1)}, u32[]{:S(2)}, u32[]{:S(2)}) collective-permute-start(f32[256,320]{0,1:T(8,128)S(1)} %collective-permute-done.1), channel_id=1, source_target_pairs={{0,224},{32,0},{64,32},{96,64},{128,96},{160,128},{192,160},{224,1... | collective-permute-start | bytes 983048 | tf_op jit(solution)/shard_map/ppermute | solution.py:77
  57.4 6.5 %collective-permute-done.2 = f32[256,320]{0,1:T(8,128)S(1)} collective-permute-done((f32[256,320]{0,1:T(8,128)S(1)}, f32[256,320]{0,1:T(8,128)S(1)}, u32[]{:S(2)}, u32[]{:S(2)}) %collective-permute-start.2) | collective-permute-done | bytes 327712 | tf_op jit(solution)/shard_map/ppermute | solution.py:72
  63.9 0.0 collective-permute-start.4
  63.9 0.8 constant_dynamic-update-slice_fusion.6
  64.7 0.8 constant_dynamic-update-slice_fusion.5
  65.5 0.0 collective-permute-done.3
  65.5 2.7 %collective-permute-start.5 = (f32[256,320]{0,1:T(8,128)S(1)}, f32[256,320]{0,1:T(8,128)S(1)}, u32[]{:S(2)}, u32[]{:S(2)}) collective-permute-start(f32[256,320]{0,1:T(8,128)S(1)} %collective-permute-done.3), channel_id=1, source_target_pairs={{0,224},{32,0},{64,32},{96,64},{128,96},{160,128},{192,160},{224,1... | collective-permute-start | bytes 983048 | tf_op jit(solution)/shard_map/ppermute | solution.py:77
  68.2 0.8 constant_dynamic-update-slice_fusion.4
  69.0 3.2 %collective-permute-done.4 = f32[256,320]{0,1:T(8,128)S(1)} collective-permute-done((f32[256,320]{0,1:T(8,128)S(1)}, f32[256,320]{0,1:T(8,128)S(1)}, u32[]{:S(2)}, u32[]{:S(2)}) %collective-permute-start.4) | collective-permute-done | bytes 327712 | tf_op jit(solution)/shard_map/ppermute | solution.py:72
  72.2 0.0 collective-permute-start.6
  72.2 0.8 constant_dynamic-update-slice_fusion.3
  73.0 0.8 constant_dynamic-update-slice_fusion.2
  73.7 0.0 collective-permute-done.5
  73.7 0.8 constant_dynamic-update-slice_fusion.1
  74.5 4.8 %collective-permute-done.6 = f32[256,320]{0,1:T(8,128)S(1)} collective-permute-done((f32[256,320]{0,1:T(8,128)S(1)}, f32[256,320]{0,1:T(8,128)S(1)}, u32[]{:S(2)}, u32[]{:S(2)}) %collective-permute-start.6) | collective-permute-done | bytes 327712 | tf_op jit(solution)/shard_map/ppermute | solution.py:72
  79.3 0.8 constant_dynamic-update-slice_fusion
  80.1 4.1 %fusion.20 = f32[256,192]{0,1:T(8,128)S(1)} fusion(f32[256,2304]{1,0:T(8,128)} %all-gather.2.cloned.1.call-done, f32[2304,192]{0,1:T(8,128)S(1)} %copy-done), kind=kOutput, calls=%fused_computation.39 | convolution fusion | flops 1358954496 | bytes 4325376 | tf_op jit(solution)/shard_map/dot_general | solution.py:39
  84.3 2.9 %fusion.10 = f32[256,2048]{1,0:T(8,128)S(1)} fusion(f32[2048,320]{0,1:T(8,128)} %constant_dynamic-update-slice_fusion, f32[256,192]{0,1:T(8,128)S(1)} %fusion.20), kind=kOutput, calls=%fused_computation.14 | convolution fusion | flops 402653184 | bytes 2686976 | tf_op jit(solution)/shard_map/dot_general | solution.py:39
  87.2 3.5 %fusion.19 = (f32[256]{0:T(256)S(1)}, f32[256,2048]{1,0:T(8,128)S(1)}) fusion(f32[256,2048]{1,0:T(8,128)S(1)} %fusion.10, f32[2048,320]{0,1:T(8,128)} %constant_dynamic-update-slice_fusion, f32[256,192]{0,1:T(8,128)S(1)} %fusion.20, s32[256]{0:T(256)S(1)} %iota_add_fusion), kind=kOutput, calls=%fused_computation.38 | convolution fusion | flops 807927552 | bytes 5376000 | tf_op jit(solution)/shard_map/dot_general | solution.py:39
  90.7 0.6 fusion.2
  91.3 0.0 copy-start.1
  91.3 3.5 %fusion.4 = f32[256,128]{1,0:T(8,128)S(1)} fusion(f32[256,2048]{1,0:T(8,128)S(1)} %get-tuple-element.8, f32[2048,320]{0,1:T(8,128)} %constant_dynamic-update-slice_fusion, f32[256]{0:T(256)S(1)} %broadcast_maximum_fusion, s32[256]{0:T(256)S(1)} %iota_add_fusion, f32[256]{0:T(256)S(1)} %fusion.2), kind=kOutput, calls=%fused_computation.8 | convolution fusion | flops 806912000 | bytes 3279872 | tf_op jit(solution)/shard_map/dot_general | solution.py:39
  94.9 2.0 %convolution_bitcast_fusion = f32[32,8,2304]{2,1,0:T(8,128)S(1)} fusion(f32[256,128]{1,0:T(8,128)S(1)} %fusion.4, f32[128,2304]{1,0:T(8,128)S(1)} %copy-done.1), kind=kOutput, calls=%fused_computation | convolution fusion | flops 905969664 | bytes 3670016 | tf_op jit(solution)/shard_map/dot_general | solution.py:39
  96.9 42.1 %all_to_all.10 = f32[32,8,2304]{2,1,0:T(8,128)} all-to-all(f32[32,8,2304]{2,1,0:T(8,128)S(1)} %convolution_bitcast_fusion), channel_id=1, replica_groups=mesh['ctx'=8,'head'=32] {'head'}, dimensions={0} | all-to-all | bytes 4718592 | tf_op jit(solution)/shard_map/all_to_all | solution.py:34
  139.0 2.4 %reduce_sum.29 = f32[8,2304]{1,0:T(8,128)} reduce(f32[32,8,2304]{2,1,0:T(8,128)} %all_to_all.10, f32[]{:T(128)} %constant.61.clone.1), dimensions={0}, to_apply=%region_3.4 | reduce | flops 571392 | bytes 2433028 | tf_op jit(solution)/shard_map/reduce_sum | solution.py:35
  (11 shorter events, 0.1 us)
Async XLA Ops:
  6.5 73.6 %copy-start = (f32[2304,192]{0,1:T(8,128)S(1)}, f32[2304,192]{0,1:T(8,128)}, u32[]{:S(2)}) copy-start(f32[2304,192]{0,1:T(8,128)} %param.8) | copy-start | bytes 5308420
  6.5 73.6 %all-gather.2.cloned.1.call-start = ((), (), s32[]{:S(2)}) async-start(), calls=%async_computation.2 | async-start | bytes 2433024 | tf_op jit(solution)/shard_map/all_gather | solution.py:52
  7.3 7.0 %copy-start.4 = (f32[512]{0:T(512)S(1)}, f32[512]{0:T(512)}, u32[]{:S(2)}) copy-start(f32[512]{0:T(512)} %param.10) | copy-start | bytes 6148
  14.1 23.5 %copy-start.2 = (f32[512,128]{1,0:T(8,128)S(1)}, f32[512,128]{1,0:T(8,128)}, u32[]{:S(2)}) copy-start(f32[512,128]{1,0:T(8,128)} %param.12) | copy-start | bytes 786436
  14.1 24.1 %copy-start.3 = (f32[512,128]{1,0:T(8,128)S(1)}, f32[512,128]{1,0:T(8,128)}, u32[]{:S(2)}) copy-start(f32[512,128]{1,0:T(8,128)} %param.11) | copy-start | bytes 786436
  15.3 22.3 %all-to-all-start = ((f32[32,8,576]{2,1,0:T(8,128)}), f32[32,8,576]{2,1,0:T(8,128)S(1)}, u32[]{:S(2)}, u32[]{:S(2)}) async-start(f32[32,8,576]{2,1,0:T(8,128)} %broadcast_in_dim.23), calls=%async_computation | async-start | bytes 1310720 | tf_op jit(solution)/shard_map/all_to_all | solution.py:19
  41.6 13.2 %collective-permute-start = (f32[256,320]{0,1:T(8,128)S(1)}, f32[256,320]{0,1:T(8,128)S(1)}, u32[]{:S(2)}, u32[]{:S(2)}) collective-permute-start(f32[256,320]{0,1:T(8,128)S(1)} %get-tuple-element.5), channel_id=1, source_target_pairs={{0,32},{32,64},{64,96},{96,128},{128,160},{160,192},{192,224},{224... | collective-permute-start | bytes 983048 | tf_op jit(solution)/shard_map/ppermute | solution.py:72
  43.2 11.6 %collective-permute-start.1 = (f32[256,320]{0,1:T(8,128)S(1)}, f32[256,320]{0,1:T(8,128)S(1)}, u32[]{:S(2)}, u32[]{:S(2)}) collective-permute-start(f32[256,320]{0,1:T(8,128)S(1)} %get-tuple-element.5), channel_id=1, source_target_pairs={{0,224},{32,0},{64,32},{96,64},{128,96},{160,128},{192,160},{224,1... | collective-permute-start | bytes 983048 | tf_op jit(solution)/shard_map/ppermute | solution.py:77
  54.7 9.2 %collective-permute-start.2 = (f32[256,320]{0,1:T(8,128)S(1)}, f32[256,320]{0,1:T(8,128)S(1)}, u32[]{:S(2)}, u32[]{:S(2)}) collective-permute-start(f32[256,320]{0,1:T(8,128)S(1)} %collective-permute-done), channel_id=1, source_target_pairs={{0,32},{32,64},{64,96},{96,128},{128,160},{160,192},{192,224},{224... | collective-permute-start | bytes 983048 | tf_op jit(solution)/shard_map/ppermute | solution.py:72
  54.7 10.8 %collective-permute-start.3 = (f32[256,320]{0,1:T(8,128)S(1)}, f32[256,320]{0,1:T(8,128)S(1)}, u32[]{:S(2)}, u32[]{:S(2)}) collective-permute-start(f32[256,320]{0,1:T(8,128)S(1)} %collective-permute-done.1), channel_id=1, source_target_pairs={{0,224},{32,0},{64,32},{96,64},{128,96},{160,128},{192,160},{224,1... | collective-permute-start | bytes 983048 | tf_op jit(solution)/shard_map/ppermute | solution.py:77
  63.9 8.3 %collective-permute-start.4 = (f32[256,320]{0,1:T(8,128)S(1)}, f32[256,320]{0,1:T(8,128)S(1)}, u32[]{:S(2)}, u32[]{:S(2)}) collective-permute-start(f32[256,320]{0,1:T(8,128)S(1)} %collective-permute-done.2), channel_id=1, source_target_pairs={{0,32},{32,64},{64,96},{96,128},{128,160},{160,192},{192,224},{224... | collective-permute-start | bytes 983048 | tf_op jit(solution)/shard_map/ppermute | solution.py:72
  65.5 8.2 %collective-permute-start.5 = (f32[256,320]{0,1:T(8,128)S(1)}, f32[256,320]{0,1:T(8,128)S(1)}, u32[]{:S(2)}, u32[]{:S(2)}) collective-permute-start(f32[256,320]{0,1:T(8,128)S(1)} %collective-permute-done.3), channel_id=1, source_target_pairs={{0,224},{32,0},{64,32},{96,64},{128,96},{160,128},{192,160},{224,1... | collective-permute-start | bytes 983048 | tf_op jit(solution)/shard_map/ppermute | solution.py:77
  72.2 7.1 %collective-permute-start.6 = (f32[256,320]{0,1:T(8,128)S(1)}, f32[256,320]{0,1:T(8,128)S(1)}, u32[]{:S(2)}, u32[]{:S(2)}) collective-permute-start(f32[256,320]{0,1:T(8,128)S(1)} %collective-permute-done.4), channel_id=1, source_target_pairs={{0,32},{32,64},{64,96},{96,128},{128,160},{160,192},{192,224},{224... | collective-permute-start | bytes 983048 | tf_op jit(solution)/shard_map/ppermute | solution.py:72
  91.3 3.5 %copy-start.1 = (f32[128,2304]{1,0:T(8,128)S(1)}, f32[128,2304]{1,0:T(8,128)}, u32[]{:S(2)}) copy-start(f32[128,2304]{1,0:T(8,128)} %param.13) | copy-start | bytes 3538948
Sparse Core Ops, SparseCore 0:
  9.9 56.1 all-gather.1
